TPU v7x, 32 devices: a whole 2x2x4 slice. The times are simulated.
32 devices in a mesh: real: 2 (over y), comp: 4 (over z), space: 4 (over x, core).
Axes of the slice: x: 2, y: 2, z: 4, core: 2. Of those that a mesh axis runs over, the one named last changes fastest.
Arguments:
- concentration: float32 [256, 32, 2048], P(('real', 'comp'), None, 'space'), parts along dimension 0, may hold values from -12 to 12
- face_rate: float32 [2, 64, 2048], P(None, 'real', 'space'), parts along dimension 1, may hold values from 0.02 to 0.15
- face_flag: int32 [2, 64, 2048], P(None, 'real', 'space'), parts along dimension 1, may hold values from 0 to 1
- retardation: float32 [16], replicated, may hold values from 1 to 3
- dispersion: float32 [16], replicated, may hold values from 0.01 to 0.08
- mixing: float32 [16, 16], replicated, may hold values from -0.08 to 2.5
- mixing_inverse: float32 [16, 16], replicated, may hold values from -0.05 to 0.5
- affinity: float32 [16], replicated, may hold values from 0.5 to 3
- mineral: float32 [16], replicated, may hold values from 0.3 to 1.5
- stiff_mask: int32 [8, 64, 2048], P(None, ('real', 'comp'), 'space'), parts along dimension 1, may hold values from 0 to 1, as said below
Outputs:
- concentration_out: float32 [256, 32, 2048], P(('real', 'comp'), None, 'space'), parts along dimension 0
There are 2 independent parts, one for each index of `real`. A program takes and returns all parts, laid end to end along the dimension named above; an argument that names none is the same for every part. Nothing has to cross between parts.
Inputs may be any that keep to these rules, and one draw needn't show every extreme that they name: `stiff_mask`: in every block of cells made of all 8 layers, x rows k * 8 to (k + 1) * 8 - 1 and y columns l * 512 to (l + 1) * 512 - 1, at most 8192 cells are stiff, and some block has exactly 8192.
All inputs are finite; a program needn't handle non-finite values.
Results may differ from a plain program's by a relative error of at most 0.00011.
Values sent between devices are 32-bit elements; how exact they have to be, the bound alone decides.
A program may use at most 64 MiB of HBM per device.

v0:
```python
import functools

import jax
import jax.numpy as jnp
from jax import lax
from jax.experimental import pallas as pl
from jax.experimental.pallas import tpu as pltpu
from jax.sharding import PartitionSpec as P

NC = 16
NZ = 8
STEPS = 2
NEWT = 4
STIFF = 4
LANES = 128
AHEAD = 3
BEHIND = 2
MESH = pl.DeviceIdType.MESH

highest = lax.Precision.HIGHEST


def split(value):
    high = value.astype(jnp.bfloat16)
    low = (value - high.astype(jnp.float32)).astype(jnp.bfloat16)
    return high, low


def expand(small, rows):
    count = small.shape[0]
    size = count * rows
    tall = (
        lax.broadcasted_iota(jnp.int32, (size, count), 0) // rows
        == lax.broadcasted_iota(jnp.int32, (size, count), 1)
    ).astype(jnp.float32)
    wide = (
        lax.broadcasted_iota(jnp.int32, (count, size), 1) // rows
        == lax.broadcasted_iota(jnp.int32, (count, size), 0)
    ).astype(jnp.float32)
    dot = functools.partial(jnp.dot, precision=highest, preferred_element_type=jnp.float32)
    full = dot(dot(tall, small), wide)
    same = (
        lax.broadcasted_iota(jnp.int32, (size, size), 0) % rows
        == lax.broadcasted_iota(jnp.int32, (size, size), 1) % rows
    )
    return jnp.where(same, full, 0.0)


def shift_cols(values, left, right):
    columns = values.shape[1]
    lower = pltpu.roll(jnp.concatenate([left, values], axis=1), 1, 1)[:, LANES:]
    upper = pltpu.roll(
        jnp.concatenate([values, right], axis=1), columns + LANES - 1, 1
    )[:, :columns]
    return lower, upper


def stencil(values, lower_row, upper_row, lower_col, upper_col, coefs, spread, retard):
    inverse = 1.0 / jnp.full((1, values.shape[1]), retard, jnp.float32)
    moved = (
        (coefs[0] + spread) * lower_row
        + (coefs[1] + spread) * upper_row
        + (coefs[2] + spread) * lower_col
        + (coefs[3] + spread) * upper_col
        - (coefs[4] + 4.0 * spread) * values
    )
    return values + moved * inverse


def fused_kernel(
    n,
    wide,
    conc,
    rate,
    flag,
    retard,
    spread,
    mixing,
    inverse,
    affinity,
    mineral,
    mask,
    out,
    moved,
    cell,
    first,
    second,
    xsend,
    xrecv,
    yone,
    ytwo,
    rim_rate,
    rim_flag,
    coefs,
    weights_in,
    weights_one,
    weights_two,
    target,
    state,
    base,
    kept,
    in_send,
    in_recv,
    out_send,
    out_recv,
    x_send,
    x_recv,
    y1_send,
    y1_recv,
    y2_send,
    y2_recv,
    r_send,
    r_recv,
):
    own, layers, nx, ny = conc.shape
    rows = mask.shape[1]
    me = lax.axis_index("comp")
    side = lax.axis_index("space")
    has_left, has_right = side > 0, side < wide - 1
    has_low, has_up = me > 0, me < n - 1
    my_rows = pl.ds(pl.multiple_of(me * rows, rows), rows)

    def peer(d):
        return lax.rem(me + d, n)

    def remote(src, dst, send, recv, **where):
        return pltpu.make_async_remote_copy(
            src_ref=src, dst_ref=dst, send_sem=send, recv_sem=recv,
            device_id=where, device_id_type=MESH,
        )

    def y1_copy(z, way):
        source = conc.at[:, z, :, pl.ds(ny - LANES if way == 0 else 0, LANES)]
        return remote(source, yone.at[way, :, z], y1_send.at[way, z], y1_recv.at[way, z],
                      space=side + (1 if way == 0 else -1))

    def y2_copy(z, way):
        source = first.at[:, z, :, pl.ds(ny - LANES if way == 0 else 0, LANES)]
        return remote(source, ytwo.at[way, :, z], y2_send.at[way, z], y2_recv.at[way, z],
                      space=side + (1 if way == 0 else -1))

    def x_copy(z, way):
        return remote(xsend.at[way, z], xrecv.at[way, z], x_send.at[way, z], x_recv.at[way, z],
                      comp=me + (1 if way == 0 else -1))

    def rim_copies():
        last = pl.ds(ny - LANES, LANES)
        return (
            remote(rate.at[1, :, last], rim_rate, r_send.at[0], r_recv.at[0], space=side + 1),
            remote(flag.at[1, :, last], rim_flag, r_send.at[1], r_recv.at[1], space=side + 1),
        )

    def in_copy(z, d):
        to = peer(d)
        source = moved.at[:, z, pl.ds(pl.multiple_of(to * rows, rows), rows), :]
        return remote(source, cell.at[pl.ds(me * own, own), z],
                      in_send.at[z, d - 1], in_recv.at[z, d - 1], comp=to)

    def in_arrival(z, d):
        source = moved.at[:, z, my_rows, :]
        return remote(source, cell.at[pl.ds(peer(n - d) * own, own), z],
                      in_send.at[z, d - 1], in_recv.at[z, d - 1], comp=peer(d))

    def out_copy(z, d):
        to = peer(d)
        return remote(second.at[pl.ds(to * own, own), z], out.at[:, z, my_rows, :],
                      out_send.at[z, d - 1], out_recv.at[z, d - 1], comp=to)

    def out_arrival(z, d):
        rows_from = pl.ds(pl.multiple_of(peer(n - d) * rows, rows), rows)
        return remote(second.at[pl.ds(me * own, own), z], out.at[:, z, rows_from, :],
                      out_send.at[z, d - 1], out_recv.at[z, d - 1], comp=peer(d))

    barrier = pltpu.get_barrier_semaphore()
    for d in range(1, n):
        pl.semaphore_signal(barrier, inc=1, device_id={"comp": peer(d)}, device_id_type=MESH)

    @pl.when(has_left)
    def _():
        pl.semaphore_signal(barrier, inc=1, device_id={"space": side - 1}, device_id_type=MESH)

    @pl.when(has_right)
    def _():
        pl.semaphore_signal(barrier, inc=1, device_id={"space": side + 1}, device_id_type=MESH)

    pl.semaphore_wait(barrier, n - 1 + has_left.astype(jnp.int32) + has_right.astype(jnp.int32))

    @pl.when(has_right)
    def _():
        for copy in rim_copies():
            copy.start()

        @pl.loop(0, layers)
        def _(z):
            y1_copy(z, 0).start()

    @pl.when(has_left)
    def _():
        @pl.loop(0, layers)
        def _(z):
            y1_copy(z, 1).start()

    @pl.when(jnp.logical_not(has_left))
    def _():
        yone[0] = jnp.zeros_like(yone[0])
        ytwo[0] = jnp.zeros_like(ytwo[0])
        rim_rate[...] = jnp.zeros_like(rim_rate)
        rim_flag[...] = jnp.zeros_like(rim_flag)

    @pl.when(jnp.logical_not(has_right))
    def _():
        yone[1] = jnp.zeros_like(yone[1])
        ytwo[1] = jnp.zeros_like(ytwo[1])

    @pl.when(jnp.logical_not(has_low))
    def _():
        xrecv[0] = jnp.zeros_like(xrecv[0])

    @pl.when(jnp.logical_not(has_up))
    def _():
        xrecv[1] = jnp.zeros_like(xrecv[1])

    @pl.when(has_left)
    def _():
        for copy in rim_copies():
            copy.wait_recv()

    flags = flag[...].astype(jnp.float32)
    plus = rate[...] * flags
    minus = rate[...] * (1.0 - flags)
    rim = rim_flag[...].astype(jnp.float32)
    rim_plus = rim_rate[...] * rim
    rim_minus = rim_rate[...] * (1.0 - rim)
    row_index = lax.broadcasted_iota(jnp.int32, (nx, ny), 0)
    down_plus = jnp.where(row_index == 0, 0.0, pltpu.roll(plus[0], 1, 0))
    down_minus = jnp.where(row_index == 0, 0.0, pltpu.roll(minus[0], 1, 0))
    side_plus = pltpu.roll(jnp.concatenate([rim_plus, plus[1]], axis=1), 1, 1)[:, LANES:]
    side_minus = pltpu.roll(jnp.concatenate([rim_minus, minus[1]], axis=1), 1, 1)[:, LANES:]
    coefs[0] = down_plus
    coefs[1] = minus[0]
    coefs[2] = side_plus
    coefs[3] = minus[1]
    coefs[4] = down_minus + plus[0] + side_minus + plus[1]

    def build_weights():
        matrix = inverse[...]
        eye = (
            lax.broadcasted_iota(jnp.int32, matrix.shape, 0)
            == lax.broadcasted_iota(jnp.int32, matrix.shape, 1)
        ).astype(jnp.float32)
        carry = eye - jnp.dot(
            matrix, mixing[...], precision=highest, preferred_element_type=jnp.float32
        )
        parts = [carry, -matrix * affinity[...], -matrix * mineral[...], matrix]
        parts = [split(expand(part, rows)) for part in parts]
        for ref, chosen in (
            (weights_one, parts[:2]),
            (weights_two, parts[:3]),
            (weights_in, parts[3:]),
        ):
            high = [part[0] for part in chosen]
            low = [part[1] for part in chosen]
            ref[...] = jnp.concatenate(high + high + low, axis=1)

    def product(ref, values):
        pairs = [split(value) for value in values]
        high = [pair[0] for pair in pairs]
        low = [pair[1] for pair in pairs]
        data = jnp.concatenate(high + low + high, axis=0)
        return jnp.dot(ref[...], data, preferred_element_type=jnp.float32)

    width = min(256, ny)
    pieces = [pl.ds(start, width) for start in range(0, ny, width)]

    def speciate(z):
        for piece in pieces:
            begun = product(weights_in, [target[:, piece]])
            base[:, piece] = begun
            state[:, piece] = begun

        @pl.loop(0, NEWT - 1)
        def _(_step):
            for piece in pieces:
                s = state[:, piece]
                state[:, piece] = base[:, piece] + product(weights_one, [s, jnp.tanh(s)])

        kept[...] = state[...]

        @pl.loop(0, STIFF)
        def _(_step):
            for piece in pieces:
                s = state[:, piece]
                state[:, piece] = base[:, piece] + product(
                    weights_two, [s, jnp.tanh(s), jnp.tanh(2.0 * s)]
                )

        stiff = mask[z] > 0
        return [
            jnp.where(stiff, state[pl.ds(c * rows, rows), :], kept[pl.ds(c * rows, rows), :])
            for c in range(NC)
        ]

    def stage_a(z):
        @pl.when(has_left)
        def _():
            y1_copy(z, 0).wait_recv()

        @pl.when(has_right)
        def _():
            y1_copy(z, 1).wait_recv()

        for c in range(own):
            u = conc[c, z]
            lower_row = jnp.where(row_index == 0, 0.0, pltpu.roll(u, 1, 0))
            upper_row = jnp.where(row_index == nx - 1, 0.0, pltpu.roll(u, nx - 1, 0))
            lower_col, upper_col = shift_cols(u, yone[0, c, z], yone[1, c, z])
            component = me * own + c
            moved[c, z] = stencil(
                u, lower_row, upper_row, lower_col, upper_col,
                [coefs[k] for k in range(5)], spread[component], retard[component],
            )
        for d in range(1, n):
            in_copy(z, d).start()

    def stage_b(z):
        for d in range(1, n):
            in_arrival(z, d).wait_recv()
        for c in range(NC):
            target[pl.ds(c * rows, rows), :] = cell[c, z]
        for c in range(own):
            spot = pl.multiple_of((me * own + c) * rows, rows)
            target[pl.ds(spot, rows), :] = moved[c, z, my_rows, :]
        done = speciate(z)
        for c in range(NC):
            first[c, z] = done[c]
            xsend[0, z, pl.ds(c, 1), :] = done[c][rows - 1 : rows]
            xsend[1, z, pl.ds(c, 1), :] = done[c][:1]

        @pl.when(has_up)
        def _():
            x_copy(z, 0).start()

        @pl.when(has_low)
        def _():
            x_copy(z, 1).start()

        @pl.when(has_right)
        def _():
            y2_copy(z, 0).start()

        @pl.when(has_left)
        def _():
            y2_copy(z, 1).start()

    def stage_c(z):
        @pl.when(has_low)
        def _():
            x_copy(z, 0).wait_recv()

        @pl.when(has_up)
        def _():
            x_copy(z, 1).wait_recv()

        @pl.when(has_left)
        def _():
            y2_copy(z, 0).wait_recv()

        @pl.when(has_right)
        def _():
            y2_copy(z, 1).wait_recv()

        local = lax.broadcasted_iota(jnp.int32, (rows, ny), 0)
        for c in range(NC):
            u = first[c, z]
            below = jnp.broadcast_to(xrecv[0, z, pl.ds(c, 1), :], u.shape)
            above = jnp.broadcast_to(xrecv[1, z, pl.ds(c, 1), :], u.shape)
            lower_row = jnp.where(local == 0, below, pltpu.roll(u, 1, 0))
            upper_row = jnp.where(local == rows - 1, above, pltpu.roll(u, rows - 1, 0))
            lower_col, upper_col = shift_cols(u, ytwo[0, c, z], ytwo[1, c, z])
            target[pl.ds(c * rows, rows), :] = stencil(
                u, lower_row, upper_row, lower_col, upper_col,
                [coefs[k, my_rows, :] for k in range(5)], spread[c], retard[c],
            )
        done = speciate(z)
        for c in range(NC):
            second[c, z] = done[c]
        for d in range(1, n):
            out_copy(z, d).start()
        for c in range(own):
            out[c, z, my_rows, :] = second[me * own + c, z]

    @pl.loop(0, layers + AHEAD + BEHIND)
    def _(i):
        @pl.when(i < layers)
        def _():
            stage_a(i)

        @pl.when(i == AHEAD - 1)
        def _():
            build_weights()

        @pl.when((i >= AHEAD) & (i < layers + AHEAD))
        def _():
            stage_b(i - AHEAD)

        @pl.when(i >= AHEAD + BEHIND)
        def _():
            stage_c(i - AHEAD - BEHIND)

    @pl.loop(0, layers)
    def _(z):
        for d in range(1, n):
            out_arrival(z, d).wait_recv()
            in_copy(z, d).wait_send()
            out_copy(z, d).wait_send()

    @pl.when(has_right)
    def _():
        for copy in rim_copies():
            copy.wait_send()

        @pl.loop(0, layers)
        def _(z):
            y1_copy(z, 0).wait_send()
            y2_copy(z, 0).wait_send()

    @pl.when(has_left)
    def _():
        @pl.loop(0, layers)
        def _(z):
            y1_copy(z, 1).wait_send()
            y2_copy(z, 1).wait_send()

    @pl.when(has_up)
    def _():
        @pl.loop(0, layers)
        def _(z):
            x_copy(z, 0).wait_send()

    @pl.when(has_low)
    def _():
        @pl.loop(0, layers)
        def _(z):
            x_copy(z, 1).wait_send()


def fused_shards(
    n, wide, concentration, face_rate, face_flag, retardation, dispersion,
    mixing, mixing_inverse, affinity, mineral, stiff_mask,
):
    planes, nx, ny = concentration.shape
    own = planes // NZ
    rows = stiff_mask.shape[1]
    size = NC * rows
    f32, bf16 = jnp.float32, jnp.bfloat16
    vmem = pl.BlockSpec(memory_space=pltpu.VMEM)
    smem = pl.BlockSpec(memory_space=pltpu.SMEM)
    dma = pltpu.SemaphoreType.DMA
    result = pl.pallas_call(
        functools.partial(fused_kernel, n, wide),
        out_shape=jax.ShapeDtypeStruct((own, NZ, nx, ny), f32),
        in_specs=[vmem, vmem, vmem, smem, smem, vmem, vmem, vmem, vmem, vmem],
        out_specs=vmem,
        scratch_shapes=[
            pltpu.VMEM((own, NZ, nx, ny), f32),
            pltpu.VMEM((NC, NZ, rows, ny), f32),
            pltpu.VMEM((NC, NZ, rows, ny), f32),
            pltpu.VMEM((NC, NZ, rows, ny), f32),
            pltpu.VMEM((2, NZ, NC, ny), f32),
            pltpu.VMEM((2, NZ, NC, ny), f32),
            pltpu.VMEM((2, own, NZ, nx, LANES), f32),
            pltpu.VMEM((2, NC, NZ, rows, LANES), f32),
            pltpu.VMEM((nx, LANES), f32),
            pltpu.VMEM((nx, LANES), jnp.int32),
            pltpu.VMEM((5, nx, ny), f32),
            pltpu.VMEM((size, 3 * size), bf16),
            pltpu.VMEM((size, 6 * size), bf16),
            pltpu.VMEM((size, 9 * size), bf16),
            pltpu.VMEM((size, ny), f32),
            pltpu.VMEM((size, ny), f32),
            pltpu.VMEM((size, ny), f32),
            pltpu.VMEM((size, ny), f32),
            dma((NZ, n - 1)), dma((NZ, n - 1)),
            dma((NZ, n - 1)), dma((NZ, n - 1)),
            dma((2, NZ)), dma((2, NZ)),
            dma((2, NZ)), dma((2, NZ)),
            dma((2, NZ)), dma((2, NZ)),
            dma((2,)), dma((2,)),
        ],
        compiler_params=pltpu.CompilerParams(collective_id=0, has_side_effects=True),
    )(
        concentration.reshape(own, NZ, nx, ny), face_rate, face_flag, retardation, dispersion,
        mixing, mixing_inverse, affinity.reshape(1, NC), mineral.reshape(1, NC), stiff_mask,
    )
    return result.reshape(planes, nx, ny)


def shifted(shard, axis, by):
    devices = lax.axis_size(axis)
    pairs = [(i, i + by) for i in range(devices) if 0 <= i + by < devices]
    return lax.ppermute(shard, axis, pairs)


def extended(block, sides, width):
    for axis, dim in sides:
        count = lax.axis_size(axis)
        forward = [(i, i + 1) for i in range(count - 1)]
        backward = [(target, source) for source, target in forward]
        low = lax.ppermute(
            lax.slice_in_dim(block, block.shape[dim] - width, None, axis=dim), axis, forward
        )
        high = lax.ppermute(lax.slice_in_dim(block, 0, width, axis=dim), axis, backward)
        block = jnp.concatenate([low, block, high], axis=dim)
    return block


def shift_down(values, axis_index):
    size_along = values.shape[axis_index]
    zero_row = jnp.zeros_like(lax.slice_in_dim(values, 0, 1, axis=axis_index))
    kept = lax.slice_in_dim(values, 0, size_along - 1, axis=axis_index)
    return jnp.concatenate([zero_row, kept], axis=axis_index)


def face_weights(face_rate, face_flag):
    flag_values = face_flag.astype(jnp.float32)
    weight_plus = face_rate * flag_values
    weight_minus = face_rate * (1.0 - flag_values)
    return (weight_plus, weight_minus)


def advance(
    values, lower_row, upper_row, lower_col, upper_col, coefficients, retard_planes, spread_planes
):
    divergence = (
        coefficients[0] * lower_row
        + coefficients[1] * upper_row
        + coefficients[2] * lower_col
        + coefficients[3] * upper_col
        - coefficients[4] * values
    )
    laplace = lower_row + upper_row + lower_col + upper_col - 4.0 * values
    return values + (divergence + spread_planes * laplace) / retard_planes


def residual_of(species, target, mixing, affinity, mineral, stiff):
    total = jnp.dot(
        mixing, species, precision=highest, preferred_element_type=jnp.float32
    ) + affinity[:, None] * jnp.tanh(species)
    if stiff:
        total = total + mineral[:, None] * jnp.tanh(2.0 * species)
    return total - target


def newton_steps(species, target, repeats, stiff, mixing, mixing_inverse, affinity, mineral):
    for iteration in range(repeats):
        update = residual_of(species, target, mixing, affinity, mineral, stiff)
        species = species - jnp.dot(
            mixing_inverse, update, precision=highest, preferred_element_type=jnp.float32
        )
    return species


def speciate(cell_block, stiff_mask, mixing, mixing_inverse, affinity, mineral):
    target = cell_block.reshape(NC, -1)
    flat_mask = stiff_mask.reshape(-1) > 0
    species = jnp.zeros_like(target)
    species = newton_steps(species, target, NEWT, False, mixing, mixing_inverse, affinity, mineral)
    stiffer = newton_steps(species, target, STIFF, True, mixing, mixing_inverse, affinity, mineral)
    species = jnp.where(flat_mask[None, :], stiffer, species)
    return species.reshape(cell_block.shape)


def shards(
    concentration,
    face_rate,
    face_flag,
    retardation,
    dispersion,
    mixing,
    mixing_inverse,
    affinity,
    mineral,
    stiff_mask,
):
    weight_plus, weight_minus = face_weights(face_rate, face_flag)
    rim_weights = jnp.stack([weight_plus[1, :, -1], weight_minus[1, :, -1]])
    left_rims = shifted(rim_weights, "space", 1)
    side_plus = jnp.concatenate([left_rims[0][:, None], weight_plus[1, :, :-1]], axis=1)
    side_minus = jnp.concatenate([left_rims[1][:, None], weight_minus[1, :, :-1]], axis=1)
    down_plus = shift_down(weight_plus[0], 0)
    down_minus = shift_down(weight_minus[0], 0)
    centre = down_minus + weight_plus[0] + side_minus + weight_plus[1]
    coefficients = jnp.stack([down_plus, weight_minus[0], side_plus, weight_minus[1], centre])
    retard_all = jnp.repeat(retardation, NZ)
    spread_all = jnp.repeat(dispersion, NZ)
    rows_held = stiff_mask.shape[1]
    row_start = lax.axis_index("comp") * rows_held
    cell_coefficients = lax.dynamic_slice_in_dim(coefficients, row_start, rows_held, 1)
    retard_planes = retard_all[:, None, None]
    spread_planes = spread_all[:, None, None]
    cell_block = lax.all_to_all(concentration, "comp", split_axis=1, concat_axis=0, tiled=True)
    for step_index in range(STEPS):
        padded = extended(cell_block, (("comp", 1), ("space", 2)), 1)
        cell_block = advance(
            cell_block,
            padded[:, :-2, 1:-1],
            padded[:, 2:, 1:-1],
            padded[:, 1:-1, :-2],
            padded[:, 1:-1, 2:],
            cell_coefficients,
            retard_planes,
            spread_planes,
        )
        cell_block = speciate(cell_block, stiff_mask, mixing, mixing_inverse, affinity, mineral)
    return lax.all_to_all(cell_block, "comp", split_axis=0, concat_axis=1, tiled=True)


def solution(mesh):
    in_specs = (
        P(("real", "comp"), None, "space"),
        P(None, "real", "space"),
        P(None, "real", "space"),
        P(),
        P(),
        P(),
        P(),
        P(),
        P(),
        P(None, ("real", "comp"), "space"),
    )
    out_specs = P(("real", "comp"), None, "space")
    n, wide = mesh.shape["comp"], mesh.shape["space"]
    body = functools.partial(fused_shards, n, wide) if NC % n == 0 else shards
    return jax.shard_map(body, mesh=mesh, in_specs=in_specs, out_specs=out_specs, check_vma=False)
```

profile of v0, /device:TPU:1, one launch (start us, length us, event | category | flops | bytes accessed | tf_op | source)
XLA Modules:
  0.0 110.6 jit_solution(11224748263143710573)
XLA Ops:
  0.0 107.4 %shard_map.100 = f32[4,8,32,512]{3,2,1,0:T(8,128)} custom-call(f32[4,8,32,512]{3,2,1,0:T(8,128)} %bitcast.5, f32[2,32,512]{2,1,0:T(8,128)} %rate.1, s32[2,32,512]{2,1,0:T(8,128)} %flag.1, f32[16]{0:T(128)} %retard.1, f32[16]{0:T(128)} %spread.1, f32[16,16]{1,0:T(8,128)} %mixing.1, f32[16,16]{1,0:T(8,128)} %inverse.1, f32[1,16]{1,0:T(1,128)} %bitcast.6, ...), custom_call_target="tpu_custom_call" | custom-call | tf_op jit(solution)/shard_map/pallas_call | solution.py:459
  107.4 3.2 %copy.12 = f32[32,32,512]{2,1,0:T(8,128)} copy(f32[32,32,512]{2,1,0:T(8,128)} %bitcast.4) | data formatting | bytes 4194304
where the time goes:
time: 111 us
  Pallas kernels  107 us (96%)
  local copies, waits for them, and re-layouts  3.19 us (3%)
    pallas_call x1, Pallas kernels, fused_shards(): pl.pallas_call(functools.partial(fused_kernel, n, wide), out_shape=jax.Sh...  107 us
    unnamed x1, local copies, waits for them, and re-layouts  3.19 us

commit v1 on v0

--- a/solution.py
+++ b/solution.py
@@ -70,17 +70,21 @@
 def fused_kernel(
     n,
     wide,
-    conc,
-    rate,
-    flag,
+    conc_hbm,
+    rate_hbm,
+    flag_hbm,
     retard,
     spread,
     mixing,
     inverse,
     affinity,
     mineral,
+    mask_hbm,
+    out,
+    conc,
+    rate,
+    flag,
     mask,
-    out,
     moved,
     cell,
     first,
@@ -111,6 +115,8 @@
     y2_recv,
     r_send,
     r_recv,
+    load_sem,
+    small_sem,
 ):
     own, layers, nx, ny = conc.shape
     rows = mask.shape[1]
@@ -121,7 +127,21 @@
     my_rows = pl.ds(pl.multiple_of(me * rows, rows), rows)
 
     def peer(d):
+        if n == 4:
+            return (lax.rem(me + 2, 4), 3 - me, me + 1 - 2 * lax.rem(me, 2))[d - 1]
         return lax.rem(me + d, n)
+
+    def source_of(d):
+        return peer(d) if n == 4 else lax.rem(me + n - d, n)
+
+    def load(z):
+        return pltpu.make_async_copy(conc_hbm.at[:, z], conc.at[:, z], load_sem.at[z])
+
+    smalls = [
+        pltpu.make_async_copy(rate_hbm, rate, small_sem.at[0]),
+        pltpu.make_async_copy(flag_hbm, flag, small_sem.at[1]),
+        pltpu.make_async_copy(mask_hbm, mask, small_sem.at[2]),
+    ]
 
     def remote(src, dst, send, recv, **where):
         return pltpu.make_async_remote_copy(
@@ -130,7 +150,7 @@
         )
 
     def y1_copy(z, way):
-        source = conc.at[:, z, :, pl.ds(ny - LANES if way == 0 else 0, LANES)]
+        source = conc_hbm.at[:, z, :, pl.ds(ny - LANES if way == 0 else 0, LANES)]
         return remote(source, yone.at[way, :, z], y1_send.at[way, z], y1_recv.at[way, z],
                       space=side + (1 if way == 0 else -1))
 
@@ -146,8 +166,8 @@
     def rim_copies():
         last = pl.ds(ny - LANES, LANES)
         return (
-            remote(rate.at[1, :, last], rim_rate, r_send.at[0], r_recv.at[0], space=side + 1),
-            remote(flag.at[1, :, last], rim_flag, r_send.at[1], r_recv.at[1], space=side + 1),
+            remote(rate_hbm.at[1, :, last], rim_rate, r_send.at[0], r_recv.at[0], space=side + 1),
+            remote(flag_hbm.at[1, :, last], rim_flag, r_send.at[1], r_recv.at[1], space=side + 1),
         )
 
     def in_copy(z, d):
@@ -158,7 +178,7 @@
 
     def in_arrival(z, d):
         source = moved.at[:, z, my_rows, :]
-        return remote(source, cell.at[pl.ds(peer(n - d) * own, own), z],
+        return remote(source, cell.at[pl.ds(source_of(d) * own, own), z],
                       in_send.at[z, d - 1], in_recv.at[z, d - 1], comp=peer(d))
 
     def out_copy(z, d):
@@ -167,7 +187,7 @@
                       out_send.at[z, d - 1], out_recv.at[z, d - 1], comp=to)
 
     def out_arrival(z, d):
-        rows_from = pl.ds(pl.multiple_of(peer(n - d) * rows, rows), rows)
+        rows_from = pl.ds(pl.multiple_of(source_of(d) * rows, rows), rows)
         return remote(second.at[pl.ds(me * own, own), z], out.at[:, z, rows_from, :],
                       out_send.at[z, d - 1], out_recv.at[z, d - 1], comp=peer(d))
 
@@ -182,6 +202,13 @@
     @pl.when(has_right)
     def _():
         pl.semaphore_signal(barrier, inc=1, device_id={"space": side + 1}, device_id_type=MESH)
+
+    for copy in smalls:
+        copy.start()
+
+    @pl.loop(0, layers)
+    def _(z):
+        load(z).start()
 
     pl.semaphore_wait(barrier, n - 1 + has_left.astype(jnp.int32) + has_right.astype(jnp.int32))
 
@@ -225,6 +252,8 @@
         for copy in rim_copies():
             copy.wait_recv()
 
+    for copy in smalls:
+        copy.wait()
     flags = flag[...].astype(jnp.float32)
     plus = rate[...] * flags
     minus = rate[...] * (1.0 - flags)
@@ -309,6 +338,7 @@
         def _():
             y1_copy(z, 1).wait_recv()
 
+        load(z).wait()
         for c in range(own):
             u = conc[c, z]
             lower_row = jnp.where(row_index == 0, 0.0, pltpu.roll(u, 1, 0))
@@ -455,13 +485,18 @@
     f32, bf16 = jnp.float32, jnp.bfloat16
     vmem = pl.BlockSpec(memory_space=pltpu.VMEM)
     smem = pl.BlockSpec(memory_space=pltpu.SMEM)
+    hbm = pl.BlockSpec(memory_space=pl.ANY)
     dma = pltpu.SemaphoreType.DMA
     result = pl.pallas_call(
         functools.partial(fused_kernel, n, wide),
-        out_shape=jax.ShapeDtypeStruct((own, NZ, nx, ny), f32),
-        in_specs=[vmem, vmem, vmem, smem, smem, vmem, vmem, vmem, vmem, vmem],
+        out_shape=pltpu.VMEM((own, NZ, nx, ny), f32),
+        in_specs=[hbm, hbm, hbm, smem, smem, vmem, vmem, vmem, vmem, hbm],
         out_specs=vmem,
         scratch_shapes=[
+            pltpu.VMEM((own, NZ, nx, ny), f32),
+            pltpu.VMEM(face_rate.shape, f32),
+            pltpu.VMEM(face_flag.shape, jnp.int32),
+            pltpu.VMEM(stiff_mask.shape, jnp.int32),
             pltpu.VMEM((own, NZ, nx, ny), f32),
             pltpu.VMEM((NC, NZ, rows, ny), f32),
             pltpu.VMEM((NC, NZ, rows, ny), f32),
@@ -486,6 +521,7 @@
             dma((2, NZ)), dma((2, NZ)),
             dma((2, NZ)), dma((2, NZ)),
             dma((2,)), dma((2,)),
+            dma((NZ,)), dma((3,)),
         ],
         compiler_params=pltpu.CompilerParams(collective_id=0, has_side_effects=True),
     )(

time: 111 us -> 107 us (0.964)
  Pallas kernels: 107 us -> 105 us
  local copies, waits for them, and re-layouts: 3.19 us -> 1.32 us
    pallas_call x1, Pallas kernels: 107 us -> 105 us  [fused_shards(): pl.pallas_call(functools.partial(fused_kernel, n, wide), out_shape=pltpu....]
    unnamed x1, local copies, waits for them, and re-layouts: 3.19 us -> 1.32 us
where the time goes in v1:
time: 107 us
  Pallas kernels  105 us (98%)
  local copies, waits for them, and re-layouts  1.32 us (1%)
    pallas_call x1, Pallas kernels, fused_shards(): pl.pallas_call(functools.partial(fused_kernel, n, wide), out_shape=pltpu....  105 us

profile of v1, /device:TPU:1, one launch (start us, length us, event | category | flops | bytes accessed | tf_op | source)
XLA Modules:
  0.0 106.8 jit_solution(17179153170674627555)
XLA Ops:
  0.0 105.5 %shard_map.100 = f32[4,8,32,512]{3,2,1,0:T(8,128)S(1)} custom-call(f32[4,8,32,512]{3,2,1,0:T(8,128)} %bitcast.5, f32[2,32,512]{2,1,0:T(8,128)} %rate_hbm.1, s32[2,32,512]{2,1,0:T(8,128)} %flag_hbm.1, f32[16]{0:T(128)} %retard.1, f32[16]{0:T(128)} %spread.1, f32[16,16]{1,0:T(8,128)} %mixing.1, f32[16,16]{1,0:T(8,128)} %inverse.1, f32[1,16]{1,0:T(1,128)} %bitcast.6, ...), custom_call_target="tpu_custom_call" | custom-call | tf_op jit(solution)/shard_map/pallas_call | solution.py:490
  105.5 1.3 %copy.12 = f32[32,32,512]{2,1,0:T(8,128)} copy(f32[32,32,512]{2,1,0:T(8,128)S(1)} %bitcast.4) | data formatting | bytes 4194304

commit v2 on v1

--- a/solution.py
+++ b/solution.py
@@ -117,6 +117,8 @@
     r_recv,
     load_sem,
     small_sem,
+    edge_send,
+    edge_recv,
 ):
     own, layers, nx, ny = conc.shape
     rows = mask.shape[1]
@@ -170,16 +172,25 @@
             remote(flag_hbm.at[1, :, last], rim_flag, r_send.at[1], r_recv.at[1], space=side + 1),
         )
 
-    def in_copy(z, d):
+    whole = pl.ds(0, ny)
+    inner = pl.ds(LANES, ny - 2 * LANES)
+    edges = (pl.ds(0, LANES), pl.ds(ny - LANES, LANES))
+
+    def in_copy(z, d, columns, sems):
         to = peer(d)
-        source = moved.at[:, z, pl.ds(pl.multiple_of(to * rows, rows), rows), :]
-        return remote(source, cell.at[pl.ds(me * own, own), z],
-                      in_send.at[z, d - 1], in_recv.at[z, d - 1], comp=to)
-
-    def in_arrival(z, d):
-        source = moved.at[:, z, my_rows, :]
-        return remote(source, cell.at[pl.ds(source_of(d) * own, own), z],
-                      in_send.at[z, d - 1], in_recv.at[z, d - 1], comp=peer(d))
+        source = moved.at[:, z, pl.ds(pl.multiple_of(to * rows, rows), rows), columns]
+        return remote(source, cell.at[pl.ds(me * own, own), z, :, columns], *sems, comp=to)
+
+    def in_arrival(z, d, columns, sems):
+        source = moved.at[:, z, my_rows, columns]
+        return remote(source, cell.at[pl.ds(source_of(d) * own, own), z, :, columns],
+                      *sems, comp=peer(d))
+
+    def in_sems(z, d):
+        return in_send.at[z, d - 1], in_recv.at[z, d - 1]
+
+    def edge_sems(k, d):
+        return edge_send.at[k, d - 1], edge_recv.at[k, d - 1]
 
     def out_copy(z, d):
         to = peer(d)
@@ -210,23 +221,6 @@
     def _(z):
         load(z).start()
 
-    pl.semaphore_wait(barrier, n - 1 + has_left.astype(jnp.int32) + has_right.astype(jnp.int32))
-
-    @pl.when(has_right)
-    def _():
-        for copy in rim_copies():
-            copy.start()
-
-        @pl.loop(0, layers)
-        def _(z):
-            y1_copy(z, 0).start()
-
-    @pl.when(has_left)
-    def _():
-        @pl.loop(0, layers)
-        def _(z):
-            y1_copy(z, 1).start()
-
     @pl.when(jnp.logical_not(has_left))
     def _():
         yone[0] = jnp.zeros_like(yone[0])
@@ -246,30 +240,91 @@
     @pl.when(jnp.logical_not(has_up))
     def _():
         xrecv[1] = jnp.zeros_like(xrecv[1])
-
-    @pl.when(has_left)
-    def _():
-        for copy in rim_copies():
-            copy.wait_recv()
 
     for copy in smalls:
         copy.wait()
     flags = flag[...].astype(jnp.float32)
     plus = rate[...] * flags
     minus = rate[...] * (1.0 - flags)
-    rim = rim_flag[...].astype(jnp.float32)
-    rim_plus = rim_rate[...] * rim
-    rim_minus = rim_rate[...] * (1.0 - rim)
     row_index = lax.broadcasted_iota(jnp.int32, (nx, ny), 0)
+    column_index = lax.broadcasted_iota(jnp.int32, (nx, ny), 1)
     down_plus = jnp.where(row_index == 0, 0.0, pltpu.roll(plus[0], 1, 0))
     down_minus = jnp.where(row_index == 0, 0.0, pltpu.roll(minus[0], 1, 0))
-    side_plus = pltpu.roll(jnp.concatenate([rim_plus, plus[1]], axis=1), 1, 1)[:, LANES:]
-    side_minus = pltpu.roll(jnp.concatenate([rim_minus, minus[1]], axis=1), 1, 1)[:, LANES:]
+    side_plus = jnp.where(column_index == 0, 0.0, pltpu.roll(plus[1], 1, 1))
+    side_minus = jnp.where(column_index == 0, 0.0, pltpu.roll(minus[1], 1, 1))
     coefs[0] = down_plus
     coefs[1] = minus[0]
     coefs[2] = side_plus
     coefs[3] = minus[1]
     coefs[4] = down_minus + plus[0] + side_minus + plus[1]
+
+    def carry_planes(z, columns, left_of, right_of):
+        count = columns.size
+        index = lax.broadcasted_iota(jnp.int32, (nx, count), 0)
+        for c in range(own):
+            u = conc[c, z, :, columns]
+            lower_row = jnp.where(index == 0, 0.0, pltpu.roll(u, 1, 0))
+            upper_row = jnp.where(index == nx - 1, 0.0, pltpu.roll(u, nx - 1, 0))
+            lower_col, upper_col = shift_cols(u, left_of(c), right_of(c))
+            component = me * own + c
+            moved[c, z, :, columns] = stencil(
+                u, lower_row, upper_row, lower_col, upper_col,
+                [coefs[k, :, columns] for k in range(5)], spread[component], retard[component],
+            )
+
+    def carry_inner(z):
+        carry_planes(
+            z, inner,
+            lambda c: conc[c, z, :, pl.ds(0, LANES)],
+            lambda c: conc[c, z, :, pl.ds(ny - LANES, LANES)],
+        )
+
+    def carry_edges(z):
+        carry_planes(
+            z, edges[0],
+            lambda c: yone[0, c, z],
+            lambda c: conc[c, z, :, pl.ds(LANES, LANES)],
+        )
+        carry_planes(
+            z, edges[1],
+            lambda c: conc[c, z, :, pl.ds(ny - 2 * LANES, LANES)],
+            lambda c: yone[1, c, z],
+        )
+
+    load(0).wait()
+    carry_inner(0)
+
+    pl.semaphore_wait(barrier, n - 1 + has_left.astype(jnp.int32) + has_right.astype(jnp.int32))
+
+    @pl.when(has_right)
+    def _():
+        for copy in rim_copies():
+            copy.start()
+
+        @pl.loop(0, layers)
+        def _(z):
+            y1_copy(z, 0).start()
+
+    @pl.when(has_left)
+    def _():
+        @pl.loop(0, layers)
+        def _(z):
+            y1_copy(z, 1).start()
+
+    for d in range(1, n):
+        in_copy(0, d, inner, in_sems(0, d)).start()
+
+    @pl.when(has_left)
+    def _():
+        for copy in rim_copies():
+            copy.wait_recv()
+
+    rim = rim_flag[...].astype(jnp.float32)
+    at_rim = lax.broadcasted_iota(jnp.int32, (nx, LANES), 1) == 0
+    rim_plus = pltpu.roll(rim_rate[...] * rim, 1, 1)
+    rim_minus = pltpu.roll(rim_rate[...] * (1.0 - rim), 1, 1)
+    coefs[2, :, edges[0]] = coefs[2, :, edges[0]] + jnp.where(at_rim, rim_plus, 0.0)
+    coefs[4, :, edges[0]] = coefs[4, :, edges[0]] + jnp.where(at_rim, rim_minus, 0.0)
 
     def build_weights():
         matrix = inverse[...]
@@ -329,32 +384,43 @@
             for c in range(NC)
         ]
 
+    def wait_slabs(z):
+        @pl.when(has_left)
+        def _():
+            y1_copy(z, 0).wait_recv()
+
+        @pl.when(has_right)
+        def _():
+            y1_copy(z, 1).wait_recv()
+
+    def stage_a_first():
+        wait_slabs(0)
+        carry_edges(0)
+        for d in range(1, n):
+            for k in range(2):
+                in_copy(0, d, edges[k], edge_sems(k, d)).start()
+
     def stage_a(z):
-        @pl.when(has_left)
-        def _():
-            y1_copy(z, 0).wait_recv()
-
-        @pl.when(has_right)
-        def _():
-            y1_copy(z, 1).wait_recv()
-
         load(z).wait()
-        for c in range(own):
-            u = conc[c, z]
-            lower_row = jnp.where(row_index == 0, 0.0, pltpu.roll(u, 1, 0))
-            upper_row = jnp.where(row_index == nx - 1, 0.0, pltpu.roll(u, nx - 1, 0))
-            lower_col, upper_col = shift_cols(u, yone[0, c, z], yone[1, c, z])
-            component = me * own + c
-            moved[c, z] = stencil(
-                u, lower_row, upper_row, lower_col, upper_col,
-                [coefs[k] for k in range(5)], spread[component], retard[component],
-            )
+        carry_inner(z)
+        wait_slabs(z)
+        carry_edges(z)
         for d in range(1, n):
-            in_copy(z, d).start()
+            in_copy(z, d, whole, in_sems(z, d)).start()
 
     def stage_b(z):
-        for d in range(1, n):
-            in_arrival(z, d).wait_recv()
+        @pl.when(z == 0)
+        def _():
+            for d in range(1, n):
+                in_arrival(0, d, inner, in_sems(0, d)).wait_recv()
+                for k in range(2):
+                    in_arrival(0, d, edges[k], edge_sems(k, d)).wait_recv()
+
+        @pl.when(z > 0)
+        def _():
+            for d in range(1, n):
+                in_arrival(z, d, whole, in_sems(z, d)).wait_recv()
+
         for c in range(NC):
             target[pl.ds(c * rows, rows), :] = cell[c, z]
         for c in range(own):
@@ -421,7 +487,11 @@
 
     @pl.loop(0, layers + AHEAD + BEHIND)
     def _(i):
-        @pl.when(i < layers)
+        @pl.when(i == 0)
+        def _():
+            stage_a_first()
+
+        @pl.when((i > 0) & (i < layers))
         def _():
             stage_a(i)
 
@@ -441,8 +511,17 @@
     def _(z):
         for d in range(1, n):
             out_arrival(z, d).wait_recv()
-            in_copy(z, d).wait_send()
             out_copy(z, d).wait_send()
+
+    for d in range(1, n):
+        in_copy(0, d, inner, in_sems(0, d)).wait_send()
+        for k in range(2):
+            in_copy(0, d, edges[k], edge_sems(k, d)).wait_send()
+
+    @pl.loop(1, layers)
+    def _(z):
+        for d in range(1, n):
+            in_copy(z, d, whole, in_sems(z, d)).wait_send()
 
     @pl.when(has_right)
     def _():
@@ -479,6 +558,11 @@
     mixing, mixing_inverse, affinity, mineral, stiff_mask,
 ):
     planes, nx, ny = concentration.shape
+    if NC % n or ny < 4 * LANES:
+        return shards(
+            concentration, face_rate, face_flag, retardation, dispersion,
+            mixing, mixing_inverse, affinity, mineral, stiff_mask,
+        )
     own = planes // NZ
     rows = stiff_mask.shape[1]
     size = NC * rows
@@ -522,6 +606,7 @@
             dma((2, NZ)), dma((2, NZ)),
             dma((2,)), dma((2,)),
             dma((NZ,)), dma((3,)),
+            dma((2, n - 1)), dma((2, n - 1)),
         ],
         compiler_params=pltpu.CompilerParams(collective_id=0, has_side_effects=True),
     )(
@@ -666,5 +751,5 @@
     )
     out_specs = P(("real", "comp"), None, "space")
     n, wide = mesh.shape["comp"], mesh.shape["space"]
-    body = functools.partial(fused_shards, n, wide) if NC % n == 0 else shards
+    body = functools.partial(fused_shards, n, wide)
     return jax.shard_map(body, mesh=mesh, in_specs=in_specs, out_specs=out_specs, check_vma=False)

time: 107 us -> 105 us (0.981)
    pallas_call x1, Pallas kernels: 105 us -> 104 us  [fused_shards(): pl.pallas_call(functools.partial(fused_kernel, n, wide), out_shape=pltpu....]
where the time goes in v2:
time: 105 us
  Pallas kernels  104 us (99%)
  local copies, waits for them, and re-layouts  1.32 us (1%)
    pallas_call x1, Pallas kernels, fused_shards(): pl.pallas_call(functools.partial(fused_kernel, n, wide), out_shape=pltpu....  104 us

profile of v2, /device:TPU:1, one launch (start us, length us, event | category | flops | bytes accessed | tf_op | source)
XLA Modules:
  0.0 105.0 jit_solution(13936504384713507832)
XLA Ops:
  0.0 103.7 %shard_map.100 = f32[4,8,32,512]{3,2,1,0:T(8,128)S(1)} custom-call(f32[4,8,32,512]{3,2,1,0:T(8,128)} %bitcast.5, f32[2,32,512]{2,1,0:T(8,128)} %rate_hbm.1, s32[2,32,512]{2,1,0:T(8,128)} %flag_hbm.1, f32[16]{0:T(128)} %retard.1, f32[16]{0:T(128)} %spread.1, f32[16,16]{1,0:T(8,128)} %mixing.1, f32[16,16]{1,0:T(8,128)} %inverse.1, f32[1,16]{1,0:T(1,128)} %bitcast.6, ...), custom_call_target="tpu_custom_call" | custom-call | tf_op jit(solution)/shard_map/pallas_call | solution.py:574
  103.7 1.3 %copy.12 = f32[32,32,512]{2,1,0:T(8,128)} copy(f32[32,32,512]{2,1,0:T(8,128)S(1)} %bitcast.4) | data formatting | bytes 4194304
